TPU v7x, 256 devices: a whole 4x4x8 slice. The times are simulated.
256 devices in a mesh: leaf: 32 (over x_hi, z, core), head: 8 (over x_lo, y).
Axes of the slice: x: 4 (x_hi: 2, x_lo: 2; x = x_hi * 2 + x_lo), y: 4, z: 8, core: 2. Of those that a mesh axis runs over, the one named last changes fastest.
Arguments:
- latents: bfloat16 [2048, 512], P('leaf'), may hold values from -14 to 14
- queries: bfloat16 [4096, 64, 128], P('leaf', 'head'), may hold values from -14 to 14
- grad_out: bfloat16 [4096, 64, 128], P('leaf', 'head'), may hold values from -6 to 6
- key_up_matrix: bfloat16 [64, 128, 512], P('head'), may hold values from -0.25 to 0.25
- value_up_matrix: bfloat16 [64, 512, 128], P('head'), may hold values from -0.25 to 0.25
- parents: int32 [256], replicated, may hold values from 0 to 254, as said below
- branch_node: int32 [32, 8], P('leaf'), may hold values from 0 to 255
- branch_lengths: int32 [32, 8], P('leaf'), may hold values from 1 to 40, 128 in all within a row
Outputs:
- d_queries: bfloat16 [4096, 64, 128], P('leaf', 'head')
- d_latents: float32 [2048, 512], P('leaf')
Inputs may be any that keep to these rules, and one draw needn't show every extreme that they name: parents[0] = 0 and parents[n] < n for every n >= 1.
All inputs are finite; a program needn't handle non-finite values.
Results may differ from a plain program's by a relative error of at most 0.025.
The roundings to bfloat16 on the way count: a program that leaves them out, or rounds other values in their place, can miss the bound.
Values may be sent and summed in bfloat16 or wider, within the bound.
A program may use at most 64 MiB of HBM per device.

v0:
```python
import jax
import jax.numpy as jnp
from jax import lax
from jax.sharding import PartitionSpec as P

NODE_LEN = 8
softmax_scale = 192.0 ** (-0.5)
masked_score = -1e30


def ancestry(parents):
    node_count = parents.shape[0]
    indices = jnp.arange(node_count, dtype=jnp.int32)
    linked = (parents[:, None] == indices[None, :]) | (indices[:, None] == indices[None, :])
    closure = linked.astype(jnp.float32)
    for squaring in range(node_count.bit_length()):
        closure = jnp.minimum(jnp.dot(closure, closure, precision=lax.Precision.HIGHEST), 1.0)
    return closure


def token_nodes(lengths_row, nodes_row, tok_count):
    bounds = jnp.cumsum(lengths_row)
    places = jnp.arange(tok_count, dtype=jnp.int32)
    branch_of = jnp.sum((places[:, None] >= bounds[None, :]).astype(jnp.int32), axis=1)
    select = branch_of[:, None] == jnp.arange(lengths_row.shape[0], dtype=jnp.int32)[None, :]
    return jnp.sum(jnp.where(select, nodes_row[None, :], 0), axis=1)


def live_keys(node_list, closure):
    node_count = closure.shape[0]
    select = (node_list[:, None] == jnp.arange(node_count, dtype=jnp.int32)[None, :]).astype(
        jnp.float32
    )
    reached = jnp.dot(select, closure, precision=lax.Precision.HIGHEST) > 0.5
    return jnp.repeat(reached, NODE_LEN, axis=1)


def on_device(
    latents, queries, grad_out, key_up_matrix, value_up_matrix, parents, branch_node, branch_lengths
):
    closure = ancestry(parents)
    tok_count = queries.shape[0]
    heads_here = queries.shape[1]
    width = latents.shape[1]
    node_list = token_nodes(branch_lengths[0], branch_node[0], tok_count)
    key_live = live_keys(node_list, closure)
    prefix_rows = key_live.shape[1]
    query_latent = jnp.einsum(
        "thd,hdc->thc", queries, key_up_matrix, preferred_element_type=jnp.float32
    ).astype(jnp.bfloat16)
    grad_latent = jnp.einsum(
        "thv,hcv->thc", grad_out, value_up_matrix, preferred_element_type=jnp.float32
    ).astype(jnp.bfloat16)

    def scores(block_keys):
        usable = key_live[:, None, :]
        scaled = (
            jnp.einsum("thc,kc->thk", query_latent, block_keys, preferred_element_type=jnp.float32)
            * softmax_scale
        )
        return (usable, jnp.where(usable, scaled, masked_score))

    forward_start = (
        jnp.full((tok_count, heads_here), masked_score, jnp.float32),
        jnp.zeros((tok_count, heads_here), jnp.float32),
        jnp.zeros((tok_count, heads_here, width), jnp.float32),
    )
    block_keys = lax.all_gather(latents, "leaf", axis=0, tiled=True)

    def advance(state):
        running_max, running_sum, weighted = state
        usable, logits = scores(block_keys)
        new_max = jnp.maximum(running_max, jnp.max(logits, axis=-1))
        weights = jnp.where(usable, jnp.exp(logits - new_max[..., None]), 0.0)
        weighted = jnp.einsum(
            "thk,kc->thc",
            weights.astype(jnp.bfloat16),
            block_keys,
            preferred_element_type=jnp.float32,
        )
        return (new_max, jnp.sum(weights, axis=-1), weighted)

    running_max, running_sum, weighted = advance(forward_start)
    attended = weighted / running_sum[..., None]
    log_norm = running_max + jnp.log(running_sum)
    delta = jnp.sum(grad_latent.astype(jnp.float32) * attended, axis=-1)
    backward_start = (
        jnp.zeros((tok_count, heads_here, width), jnp.float32),
        jnp.zeros((prefix_rows, width), jnp.float32),
    )
    backward_block_keys = lax.all_gather(latents, "leaf", axis=0, tiled=True)

    def advance(state):
        usable, logits = scores(backward_block_keys)
        probs = jnp.where(usable, jnp.exp(logits - log_norm[..., None]), 0.0)
        grad_weights = jnp.einsum(
            "thc,kc->thk", grad_latent, backward_block_keys, preferred_element_type=jnp.float32
        )
        grad_scores = (probs * (grad_weights - delta[..., None])).astype(jnp.bfloat16)
        query_acc = jnp.einsum(
            "thk,kc->thc", grad_scores, backward_block_keys, preferred_element_type=jnp.float32
        )
        contrib = softmax_scale * jnp.einsum(
            "thk,thc->kc", grad_scores, query_latent, preferred_element_type=jnp.float32
        )
        contrib = contrib + jnp.einsum(
            "thk,thc->kc",
            probs.astype(jnp.bfloat16),
            grad_latent,
            preferred_element_type=jnp.float32,
        )
        return (query_acc, contrib)

    query_acc, latent_grad = advance(backward_start)
    query_grad = (softmax_scale * query_acc).astype(jnp.bfloat16)
    d_queries = jnp.einsum(
        "thc,hdc->thd", query_grad, key_up_matrix, preferred_element_type=jnp.float32
    ).astype(jnp.bfloat16)
    owned_rows = lax.psum_scatter(
        latent_grad.astype(jnp.bfloat16), "leaf", scatter_dimension=0, tiled=True
    )
    d_latents = lax.psum(owned_rows, "head").astype(jnp.float32)
    return (d_queries, d_latents)


def solution(mesh):
    placed = (
        P("leaf", None),
        P("leaf", "head", None),
        P("leaf", "head", None),
        P("head", None, None),
        P("head", None, None),
        P(),
        P("leaf", None),
        P("leaf", None),
    )
    return jax.shard_map(
        on_device,
        mesh=mesh,
        in_specs=placed,
        out_specs=(P("leaf", "head", None), P("leaf", None)),
        check_vma=False,
    )
```

profile of v0, /device:TPU:4, one launch (start us, length us, event | category | flops | bytes accessed | tf_op | source)
XLA Modules:
  0.0 321.0 jit_solution(14642406166411518721)
XLA Ops:
  7.2 0.0 copy-start
  7.2 0.0 copy-start.1
  7.2 0.0 all-gather.2.cloned.1.call-start
  7.2 0.7 all-gather.2.cloned.1.call-update
  7.9 0.0 reduce-scatter.2.cloned.1.call-start
  8.0 0.8 reduce-window.8
  8.8 0.1 convert_reduce_fusion
  8.9 0.7 select_reduce_fusion
  9.6 1.0 convolution_minimum_fusion.8
  10.7 0.4 convolution_minimum_fusion.7
  11.1 0.4 convolution_minimum_fusion.6
  11.4 0.4 convolution_minimum_fusion.5
  11.8 0.4 convolution_minimum_fusion.4
  12.2 0.4 convolution_minimum_fusion.3
  12.6 0.4 convolution_minimum_fusion.2
  13.0 0.4 convolution_minimum_fusion.1
  13.4 0.4 convolution_minimum_fusion
  13.8 0.3 convolution_compare_fusion
  14.0 0.1 copy.34
  14.2 0.1 broadcast_bitcast_fusion
  14.3 0.4 copy.35
  14.7 0.0 copy-done
  14.7 1.5 fusion.23
  16.2 0.0 copy-done.1
  16.2 2.4 fusion.24
  18.6 0.0 copy-start.2
  18.6 72.7 %all-gather.2.cloned.1.call-done = bf16[2048,512]{1,0:T(8,128)(2,1)} async-done(((bf16[64,512]{1,0:T(8,128)(2,1)}), bf16[2048,512]{1,0:T(8,128)(2,1)}) %all-gather.2.cloned.1.call-update) | async-done | bytes 2097168 | tf_op jit(solution)/shard_map/all_gather | solution.py:91
  91.3 4.5 %fusion.3 = (f32[128,8]{0,1:T(8,128)S(1)}, f32[128,8,2048]{2,0,1:T(8,128)S(1)}) fusion(pred[128,2048]{1,0:T(8,128)(4,1)S(1)} %copy.35, bf16[128,8,512]{0,2,1:T(8,128)(2,1)S(1)} %fusion.23, bf16[2048,512]{1,0:T(8,128)(2,1)} %all-gather.2.cloned.1.call-done), kind=kOutput, calls=%fused_computation.7 | convolution fusion | flops 2153774080 | bytes 11800576 | tf_op jit(solution)/shard_map/thc,kc->thk/dot_general | solution.py:58
  95.8 2.7 fusion.1
  98.5 0.0 copy-done.2
  98.5 0.0 copy-start.3
  98.5 3.3 %fusion.4 = f32[2048,512,1]{1,0,2:T(8,128)S(1)} fusion(bf16[128,8,512]{0,2,1:T(8,128)(2,1)S(1)} %copy-done.2, f32[128,8,2048]{2,0,1:T(8,128)S(1)} %get-tuple-element.9, f32[128,8]{0,1:T(8,128)S(1)} %log_add_fusion, pred[128,2048]{1,0:T(8,128)(4,1)S(1)} %copy.35), kind=kOutput, calls=%fused_computation.8 | convolution fusion | flops 2157969408 | bytes 13897728 | tf_op jit(solution)/shard_map/thk,thc->kc/dot_general | solution.py:106
  101.7 0.0 copy-done.3
  101.8 2.8 multiply_reduce_fusion
  104.6 5.5 %multiply_convert_fusion = bf16[128,8,2048]{2,0,1:T(8,128)(2,1)S(1)} fusion(f32[128,8,2048]{2,0,1:T(8,128)S(1)} %get-tuple-element.9, f32[128,8]{0,1:T(8,128)S(1)} %multiply_reduce_fusion, f32[128,8]{0,1:T(8,128)S(1)} %log_add_fusion, pred[128,2048]{1,0:T(8,128)(4,1)S(1)} %copy.35, bf16[128,8,512]{0,2,1:T(8,128)(2,1)S(1)} %copy-done.2, ...), kind=kOutput, calls=%fused_computation | convolution fusion | flops 2162163712 | bytes 15998976 | tf_op jit(solution)/shard_map/thc,kc->thk/dot_general | solution.py:96
  110.1 0.0 copy-start.4
  110.1 1.9 copy-done.4
  112.0 4.0 %fusion.6 = bf16[2048,512]{1,0:T(8,128)(2,1)} fusion(f32[2048,512,1]{1,0,2:T(8,128)S(1)} %fusion.4, bf16[128,8,2048]{2,0,1:T(8,128)(2,1)S(1)} %multiply_convert_fusion, bf16[128,8,512]{0,2,1:T(8,128)(2,1)S(1)} %fusion.23), kind=kOutput, calls=%fused_computation.10 | convolution fusion | flops 2150629376 | bytes 11534336 | tf_op jit(solution)/shard_map/thk,thc->kc/dot_general | solution.py:103
  116.0 0.0 reduce-scatter.2.cloned.1.call-update
  116.0 0.0 all-reduce.2.cloned.1.call-start
  116.1 117.2 %reduce-scatter.2.cloned.1.call-done = bf16[64,512]{1,0:T(8,128)(2,1)} async-done(((bf16[2048,512]{1,0:T(8,128)(2,1)}), bf16[64,512]{1,0:T(8,128)(2,1)}) %reduce-scatter.2.cloned.1.call-update) | async-done | bytes 65552 | tf_op jit(solution)/shard_map/reduce_scatter | solution.py:119
  233.3 0.0 all-reduce.2.cloned.1.call-update
  233.3 5.5 %fusion.31 = bf16[128,8,128]{2,0,1:T(8,128)(2,1)S(1)} fusion(bf16[8,128,512]{2,1,0:T(8,128)(2,1)S(1)} %copy-done, bf16[128,8,2048]{2,0,1:T(8,128)(2,1)} %copy-done.4, bf16[2048,512]{1,0:T(8,128)(2,1)} %all-gather.2.cloned.1.call-done), kind=kOutput, calls=%fused_computation.42 | convolution fusion | flops 2282881024 | bytes 7602176 | tf_op jit(solution)/shard_map/thc,hdc->thd/dot_general | solution.py:116
  238.8 0.9 copy.46
  239.6 73.3 %all-reduce.2.cloned.1.call-done = bf16[64,512]{1,0:T(8,128)(2,1)} async-done(((bf16[64,512]{1,0:T(8,128)(2,1)}), bf16[64,512]{1,0:T(8,128)(2,1)}) %all-reduce.2.cloned.1.call-update) | async-done | bytes 65552 | tf_op jit(solution)/shard_map/psum | solution.py:122
  313.0 1.5 convert_element_type.57
  (2 shorter events, 0.0 us)
Async XLA Ops:
  7.2 7.6 %copy-start = (bf16[8,128,512]{2,1,0:T(8,128)(2,1)S(1)}, bf16[8,128,512]{2,1,0:T(8,128)(2,1)}, u32[]{:S(2)}) copy-start(bf16[8,128,512]{2,1,0:T(8,128)(2,1)} %param.11) | copy-start | bytes 3145732
  7.2 9.0 %copy-start.1 = (bf16[8,512,128]{2,1,0:T(8,128)(2,1)S(1)}, bf16[8,512,128]{2,1,0:T(8,128)(2,1)}, u32[]{:S(2)}) copy-start(bf16[8,512,128]{2,1,0:T(8,128)(2,1)} %param.12) | copy-start | bytes 3145732
  7.2 84.1 %all-gather.2.cloned.1.call-start = ((), (), s32[]{:S(2)}) async-start(), calls=%async_computation.1 | async-start | bytes 2162688 | tf_op jit(solution)/shard_map/all_gather | solution.py:91
  7.9 225.3 %reduce-scatter.2.cloned.1.call-start = ((), (), s32[]{:S(2)}) async-start(), calls=%async_computation.2 | async-start | bytes 2162688 | tf_op jit(solution)/shard_map/reduce_scatter | solution.py:119
  18.6 79.9 %copy-start.2 = (bf16[128,8,512]{0,2,1:T(8,128)(2,1)S(1)}, bf16[128,8,512]{0,2,1:T(8,128)(2,1)}, u32[]{:S(2)}) copy-start(bf16[128,8,512]{0,2,1:T(8,128)(2,1)} %fusion.24) | copy-start | bytes 3145732
  98.5 3.3 %copy-start.3 = (bf16[2048,512]{1,0:T(8,128)(2,1)S(1)}, bf16[2048,512]{1,0:T(8,128)(2,1)}, u32[]{:S(2)}) copy-start(bf16[2048,512]{1,0:T(8,128)(2,1)} %all-gather.2.cloned.1.call-done) | copy-start | bytes 6291460
  110.1 1.9 copy-start.4
  116.0 196.9 %all-reduce.2.cloned.1.call-start = ((), (), s32[]{:S(2)}) async-start(), calls=%async_computation.3 | async-start | bytes 131072 | tf_op jit(solution)/shard_map/psum | solution.py:122
Sparse Core Ops, SparseCore 0:
  10.8 80.4 all-gather.1
  116.2 117.0 reduce-scatter.1
  236.1 76.8 all-reduce.1
where the time goes:
time: 321 us
  waiting for transfers between devices  264 us (82%)
  matrix products  33.7 us (10%)
  between operations  14 us (4%)
  other arithmetic  5.85 us (2%)
  local copies, waits for them, and re-layouts  3.47 us (1%)
    reduce_scatter x1, waiting for transfers between devices, on_device(): lax.psum_scatter(latent_grad.astype(jnp.bfloat16), 'leaf', scatter_dimens...  117 us
    psum x1, waiting for transfers between devices, on_device(): d_latents = lax.psum(owned_rows, 'head').astype(jnp.float32)  73.3 us
    all_gather x1, waiting for transfers between devices, on_device(): backward_block_keys = lax.all_gather(latents, 'leaf', axis=0, tiled=True)  72.7 us
  transfers between devices with their start and end apart: 3, of which 3 were waited for; matrix products, arithmetic and copies ran while one was open for 5% of the time, Pallas kernels for 0%

commit v1 on v0

--- a/solution.py
+++ b/solution.py
@@ -88,7 +88,8 @@
         jnp.zeros((tok_count, heads_here, width), jnp.float32),
         jnp.zeros((prefix_rows, width), jnp.float32),
     )
-    backward_block_keys = lax.all_gather(latents, "leaf", axis=0, tiled=True)
+    stack = jnp.stack([latents] * lax.axis_size("leaf"))
+    backward_block_keys = jnp.concatenate(lax.all_to_all(stack, "leaf", 0, 0), axis=0)
 
     def advance(state):
         usable, logits = scores(backward_block_keys)

time: 321 us -> 334 us (1.040)
  starting transfers between devices: 0.12 us -> 11.8 us
  waiting for transfers between devices: 264 us -> 256 us
  matrix products: 33.7 us -> 39.1 us
  local copies, waits for them, and re-layouts: 3.47 us -> 8.12 us
    all_to_all x0 -> x1, starting transfers between devices: none -> 11.7 us  [on_device(): lax.all_to_all(stack, 'leaf', 0, 0)]
    all_gather x1, waiting for transfers between devices: 72.7 us -> 64.4 us  [on_device(): block_keys = lax.all_gather(latents, 'leaf', axis=0, tiled=True)]
    dot_general x1 -> x2, matrix products: 4.49 us -> 8.58 us  [scores(): jnp.einsum('thc,kc->thk', query_latent, block_keys, preferred_element_typ...]
  transfers between devices with their start and end apart: 3 -> 4, of which waited for: 3 -> 3; matrix products, arithmetic and copies ran while one was open for 5% -> 8% of each run, Pallas kernels for 0% -> 0%
where the time goes in v1:
time: 334 us
  waiting for transfers between devices  256 us (77%)
  matrix products  39.1 us (12%)
  between operations  14 us (4%)
  starting transfers between devices  11.8 us (4%)
  local copies, waits for them, and re-layouts  8.12 us (2%)
  other arithmetic  4.55 us (1%)
    reduce_scatter x1, waiting for transfers between devices, on_device(): lax.psum_scatter(latent_grad.astype(jnp.bfloat16), 'leaf', scatter_dimens...  117 us
    psum x1, waiting for transfers between devices, on_device(): d_latents = lax.psum(owned_rows, 'head').astype(jnp.float32)  74 us
    all_gather x1, waiting for transfers between devices, on_device(): block_keys = lax.all_gather(latents, 'leaf', axis=0, tiled=True)  64.4 us
    all_to_all x1, starting transfers between devices, on_device(): lax.all_to_all(stack, 'leaf', 0, 0)  11.7 us
    dot_general x2, matrix products, scores(): jnp.einsum('thc,kc->thk', query_latent, block_keys, preferred_element_typ...  8.58 us
  transfers between devices with their start and end apart: 4, of which 3 were waited for; matrix products, arithmetic and copies ran while one was open for 8% of the time, Pallas kernels for 0%

profile of v1, /device:TPU:4, one launch (start us, length us, event | category | flops | bytes accessed | tf_op | source)
XLA Modules:
  0.0 334.1 jit_solution(7294920062852360928)
XLA Ops:
  7.2 0.0 copy-start
  7.2 0.0 copy-start.6
  7.2 0.0 copy-start.5
  7.2 0.0 all-gather.2.cloned.1.call-start
  7.2 0.7 all-gather.2.cloned.1.call-update
  7.9 2.4 stack.2
  10.4 0.0 copy-start.7
  10.4 11.7 %all-to-all-start = ((bf16[32,64,512]{2,1,0:T(8,128)(2,1)}), bf16[32,64,512]{2,1,0:T(8,128)(2,1)S(1)}, u32[]{:S(2)}, u32[]{:S(2)}) async-start(bf16[32,64,512]{2,1,0:T(8,128)(2,1)} %stack.2), calls=%async_computation | async-start | bytes 4194304 | tf_op jit(solution)/shard_map/all_to_all | solution.py:92
  22.1 0.0 reduce-scatter.2.cloned.1.call-start
  22.2 0.0 copy-done.6
  22.2 0.2 reduce-window.8
  22.4 0.1 convert_reduce_fusion
  22.4 0.0 copy-done.5
  22.4 0.3 convolution_minimum_fusion.8
  22.7 0.4 convolution_minimum_fusion.7
  23.1 0.4 convolution_minimum_fusion.6
  23.5 0.4 convolution_minimum_fusion.5
  23.9 0.4 convolution_minimum_fusion.4
  24.3 0.0 copy-done.7
  24.3 0.1 select_reduce_fusion
  24.4 0.4 convolution_minimum_fusion.3
  24.8 0.4 convolution_minimum_fusion.2
  25.2 0.4 convolution_minimum_fusion.1
  25.5 0.4 convolution_minimum_fusion
  25.9 0.3 convolution_compare_fusion
  26.2 0.1 copy.36
  26.3 0.8 broadcast_bitcast_fusion
  27.2 1.4 copy.37
  28.5 0.0 copy-done
  28.5 2.5 fusion.18
  31.0 2.7 fusion.19
  33.7 64.4 %all-gather.2.cloned.1.call-done = bf16[2048,512]{1,0:T(8,128)(2,1)} async-done(((bf16[64,512]{1,0:T(8,128)(2,1)}), bf16[2048,512]{1,0:T(8,128)(2,1)}) %all-gather.2.cloned.1.call-update) | async-done | bytes 2097168 | tf_op jit(solution)/shard_map/all_gather | solution.py:68
  98.0 4.8 %fusion = (f32[128,8]{0,1:T(8,128)S(1)}, f32[128,8,2048]{2,0,1:T(8,128)S(1)}) fusion(pred[128,2048]{1,0:T(8,128)(4,1)S(1)} %copy.37, bf16[128,8,512]{0,2,1:T(8,128)(2,1)} %fusion.18, bf16[2048,512]{1,0:T(8,128)(2,1)} %all-gather.2.cloned.1.call-done), kind=kOutput, calls=%fused_computation.4 | convolution fusion | flops 2153774080 | bytes 11800576 | tf_op jit(solution)/shard_map/thc,kc->thk/dot_general | solution.py:58
  102.8 0.0 copy-start.1
  102.9 2.7 fusion.2
  105.6 0.5 copy-done.1
  106.1 0.0 all-to-all-done
  106.1 0.0 copy-start.3
  106.1 0.0 slice-start
  106.1 3.8 %fusion.41 = f32[128,8,2048]{2,0,1:T(8,128)S(1)} fusion(bf16[128,8,512]{0,2,1:T(8,128)(2,1)} %fusion.18, bf16[2048,512,1]{1,0,2:T(8,128)(2,1)S(1)} %bitcast.63), kind=kOutput, calls=%fused_computation.64 | convolution fusion | flops 2147483648 | bytes 11534336 | tf_op jit(solution)/shard_map/thc,kc->thk/dot_general | solution.py:58
  109.9 0.0 copy-done.3
  109.9 0.0 slice-start.1
  109.9 0.0 copy-start.4
  109.9 5.0 %fusion.4 = f32[2048,512,1]{1,0,2:T(8,128)} fusion(bf16[128,8,512]{0,2,1:T(8,128)(2,1)S(1)} %copy-done.3, f32[128,8,2048]{2,0,1:T(8,128)S(1)} %fusion.41, f32[128,8]{0,1:T(8,128)S(1)} %log_add_fusion, pred[128,2048]{1,0:T(8,128)(4,1)S(1)} %copy.37), kind=kOutput, calls=%fused_computation.8 | convolution fusion | flops 2157969408 | bytes 13897728 | tf_op jit(solution)/shard_map/thk,thc->kc/dot_general | solution.py:107
  114.9 0.0 slice-done
  114.9 0.0 slice-done.1
  115.0 0.0 copy-done.4
  115.0 2.8 multiply_reduce_fusion
  117.8 0.0 copy-start.2
  117.8 0.0 copy-start.9
  117.8 5.4 %multiply_convert_fusion = bf16[128,8,2048]{2,0,1:T(8,128)(2,1)S(1)} fusion(f32[128,8,2048]{2,0,1:T(8,128)S(1)} %fusion.41, f32[128,8]{0,1:T(8,128)S(1)} %multiply_reduce_fusion, f32[128,8]{0,1:T(8,128)S(1)} %log_add_fusion, pred[128,2048]{1,0:T(8,128)(4,1)S(1)} %copy.37, bf16[128,8,512]{0,2,1:T(8,128)(2,1)S(1)} %copy-done.3, ...), kind=kOutput, calls=%fused_computation | convolution fusion | flops 2162163712 | bytes 15998976 | tf_op jit(solution)/shard_map/thc,kc->thk/dot_general | solution.py:97
  123.2 0.0 copy-start.8
  123.2 1.9 copy-done.8
  125.2 0.0 copy-done.2
  125.2 0.0 copy-done.9
  125.2 3.7 %fusion.6 = bf16[2048,512]{1,0:T(8,128)(2,1)} fusion(f32[2048,512,1]{1,0,2:T(8,128)S(1)} %copy-done.9, bf16[128,8,2048]{2,0,1:T(8,128)(2,1)S(1)} %multiply_convert_fusion, bf16[128,8,512]{0,2,1:T(8,128)(2,1)S(1)} %copy-done.2), kind=kOutput, calls=%fused_computation.10 | convolution fusion | flops 2150629376 | bytes 11534336 | tf_op jit(solution)/shard_map/thk,thc->kc/dot_general | solution.py:104
  128.9 0.0 reduce-scatter.2.cloned.1.call-update
  128.9 0.0 all-reduce.2.cloned.1.call-start
  129.0 117.4 %reduce-scatter.2.cloned.1.call-done = bf16[64,512]{1,0:T(8,128)(2,1)} async-done(((bf16[2048,512]{1,0:T(8,128)(2,1)}), bf16[64,512]{1,0:T(8,128)(2,1)}) %reduce-scatter.2.cloned.1.call-update) | async-done | bytes 65552 | tf_op jit(solution)/shard_map/reduce_scatter | solution.py:120
  246.4 0.0 all-reduce.2.cloned.1.call-update
  246.4 4.8 %fusion.22 = bf16[128,8,128]{2,0,1:T(8,128)(2,1)S(1)} fusion(bf16[8,128,512]{2,1,0:T(8,128)(2,1)S(1)} %copy-done, bf16[128,8,2048]{2,0,1:T(8,128)(2,1)} %copy-done.8, bf16[2048,512,1]{1,0,2:T(8,128)(2,1)S(1)} %bitcast.65), kind=kOutput, calls=%fused_computation.39 | convolution fusion | flops 2282881024 | bytes 7602176 | tf_op jit(solution)/shard_map/thc,hdc->thd/dot_general | solution.py:117
  251.2 0.9 copy.49
  252.1 74.0 %all-reduce.2.cloned.1.call-done = bf16[64,512]{1,0:T(8,128)(2,1)} async-done(((bf16[64,512]{1,0:T(8,128)(2,1)}), bf16[64,512]{1,0:T(8,128)(2,1)}) %all-reduce.2.cloned.1.call-update) | async-done | bytes 65552 | tf_op jit(solution)/shard_map/psum | solution.py:123
  326.1 1.5 convert_element_type.57
  (3 shorter events, 0.0 us)
Async XLA Ops:
  7.2 21.4 %copy-start = (bf16[8,128,512]{2,1,0:T(8,128)(2,1)S(1)}, bf16[8,128,512]{2,1,0:T(8,128)(2,1)}, u32[]{:S(2)}) copy-start(bf16[8,128,512]{2,1,0:T(8,128)(2,1)} %param.11) | copy-start | bytes 3145732
  7.2 15.0 %copy-start.6 = (s32[1,8]{1,0:T(1,128)S(1)}, s32[1,8]{1,0:T(1,128)}, u32[]{:S(2)}) copy-start(s32[1,8]{1,0:T(1,128)} %param.15) | copy-start | bytes 100
  7.2 15.3 %copy-start.5 = (s32[256]{0:T(256)S(1)}, s32[256]{0:T(256)}, u32[]{:S(2)}) copy-start(s32[256]{0:T(256)} %param.13) | copy-start | bytes 3076
  7.2 90.8 %all-gather.2.cloned.1.call-start = ((), (), s32[]{:S(2)}) async-start(), calls=%async_computation.2 | async-start | bytes 2162688 | tf_op jit(solution)/shard_map/all_gather | solution.py:68
  10.4 13.9 %copy-start.7 = (s32[1,8]{1,0:T(1,128)S(1)}, s32[1,8]{1,0:T(1,128)}, u32[]{:S(2)}) copy-start(s32[1,8]{1,0:T(1,128)} %param.14) | copy-start | bytes 100
  10.4 95.7 %all-to-all-start = ((bf16[32,64,512]{2,1,0:T(8,128)(2,1)}), bf16[32,64,512]{2,1,0:T(8,128)(2,1)S(1)}, u32[]{:S(2)}, u32[]{:S(2)}) async-start(bf16[32,64,512]{2,1,0:T(8,128)(2,1)} %stack.2), calls=%async_computation | async-start | bytes 4194304 | tf_op jit(solution)/shard_map/all_to_all | solution.py:92
  22.1 224.3 %reduce-scatter.2.cloned.1.call-start = ((), (), s32[]{:S(2)}) async-start(), calls=%async_computation.3 | async-start | bytes 2162688 | tf_op jit(solution)/shard_map/reduce_scatter | solution.py:120
  102.8 3.2 copy-start.1
  106.1 3.8 %copy-start.3 = (bf16[128,8,512]{0,2,1:T(8,128)(2,1)S(1)}, bf16[128,8,512]{0,2,1:T(8,128)(2,1)}, u32[]{:S(2)}) copy-start(bf16[128,8,512]{0,2,1:T(8,128)(2,1)} %fusion.19) | copy-start | bytes 3145732
  106.1 8.9 %slice-start = ((s8[8388608]{0:T(1024)(128)(4,1)}), s8[4194304]{0:T(1024)(128)(4,1)S(1)}, s32[]{:S(2)}) async-start(s8[8388608]{0:T(1024)(128)(4,1)} %bitcast.61), calls=%async_computation.5 | async-start | bytes 8388608
  109.9 5.1 %slice-start.1 = ((s8[8388608]{0:T(1024)(128)(4,1)}), s8[4194304]{0:T(1024)(128)(4,1)S(1)}, s32[]{:S(2)}) async-start(s8[8388608]{0:T(1024)(128)(4,1)} %bitcast.61), calls=%async_computation.6 | async-start | bytes 8388608
  109.9 5.1 %copy-start.4 = (bf16[2048,512]{1,0:T(8,128)(2,1)S(1)}, bf16[2048,512]{1,0:T(8,128)(2,1)}, u32[]{:S(2)}) copy-start(bf16[2048,512]{1,0:T(8,128)(2,1)} %all-gather.2.cloned.1.call-done) | copy-start | bytes 6291460
  117.8 7.4 %copy-start.2 = (bf16[128,8,512]{0,2,1:T(8,128)(2,1)S(1)}, bf16[128,8,512]{0,2,1:T(8,128)(2,1)}, u32[]{:S(2)}) copy-start(bf16[128,8,512]{0,2,1:T(8,128)(2,1)} %fusion.18) | copy-start | bytes 3145732
  117.8 7.4 %copy-start.9 = (f32[2048,512,1]{1,0,2:T(8,128)S(1)}, f32[2048,512,1]{1,0,2:T(8,128)}, u32[]{:S(2)}) copy-start(f32[2048,512,1]{1,0,2:T(8,128)} %fusion.4) | copy-start | bytes 12582916
  123.2 1.9 copy-start.8
  128.9 197.1 %all-reduce.2.cloned.1.call-start = ((), (), s32[]{:S(2)}) async-start(), calls=%async_computation.4 | async-start | bytes 131072 | tf_op jit(solution)/shard_map/psum | solution.py:123
Sparse Core Ops, SparseCore 0:
  10.8 87.1 all-gather.1
  129.1 117.2 reduce-scatter.1
  249.2 76.8 all-reduce.1
